TPU v7x, 32 devices: a whole 2x2x4 slice. The times are simulated.
32 devices in a mesh: groups: 2 (over x), lat: 16 (over z, y, core).
Axes of the slice: x: 2, y: 2, z: 4, core: 2. Of those that a mesh axis runs over, the one named last changes fastest.
Arguments:
- objects: float32 [2, 2, 8192, 1024], P(None, None, ('groups', 'lat')), parts along dimension 2, may hold values from -5 to 5
- probes: float32 [4, 2, 256, 256], P('groups'), parts along dimension 0, may hold values from -5 to 5
- x_offsets: int32 [64], P(('groups', 'lat')), parts along dimension 0, may hold values from 0 to 255
- y_offsets: int32 [64], P(('groups', 'lat')), parts along dimension 0, may hold values from 0 to 768
- modes: int32 [64], P(('groups', 'lat')), parts along dimension 0, may hold values from 0 to 1
- measured: float32 [64, 256, 256], P(('groups', 'lat')), parts along dimension 0, may hold values from 0 to 2
Outputs:
- updated: float32 [2, 2, 8192, 1024], P(None, None, ('groups', 'lat')), parts along dimension 2
There are 2 independent parts, one for each index of `groups`. A program takes and returns all parts, laid end to end along the dimension named above; each array names one. Nothing has to cross between parts.
All inputs are finite; a program needn't handle non-finite values.
Results may differ from a plain program's by a relative error of at most 0.0003.
Values sent between devices are 32-bit elements; how exact they have to be, the bound alone decides.
No kernel may reach another device: no remote copies, remote signals or barrier semaphores. Data moves between devices by JAX's collectives and lax.ppermute only.
A program may use at most 128 MiB of HBM per device.

v0:
```python
import math

import jax
import jax.numpy as jnp
from jax import lax
from jax.sharding import PartitionSpec as P

W = 256
TILE = 256
SLICES = 2
NPROBE = 2


spread_phase = 40.0
descent_rate = 1.0
highest = lax.Precision.HIGHEST


def from_behind(block, axis, distance):
    devices = range(lax.axis_size(axis))
    route = [(i - distance, i) for i in devices if i - distance in devices]
    return lax.ppermute(block, axis, route)


def kernel_phase(width):
    counter = jnp.arange(width, dtype=jnp.int32)
    folded = ((counter + width // 2) % width - width // 2).astype(jnp.float32) / width
    return spread_phase * (folded[:, None] ** 2 + folded[None, :] ** 2)


def fourier_tables(width):
    counter = jnp.arange(width, dtype=jnp.int32)
    wound = counter[:, None] * counter[None, :] % width
    angles = wound.astype(jnp.float32) * (2.0 * math.pi / width)
    scaling = 1.0 / math.sqrt(width)
    return (jnp.cos(angles) * scaling, jnp.sin(angles) * scaling)


def fourier_pair(real_part, imag_part, tables, direction):
    cosines, sines = tables
    signed = direction * sines
    last_real = jnp.einsum("pjk,kl->pjl", real_part, cosines, precision=highest) - jnp.einsum(
        "pjk,kl->pjl", imag_part, signed, precision=highest
    )
    last_imag = jnp.einsum("pjk,kl->pjl", imag_part, cosines, precision=highest) + jnp.einsum(
        "pjk,kl->pjl", real_part, signed, precision=highest
    )
    first_real = jnp.einsum("kj,pjl->pkl", cosines, last_real, precision=highest) - jnp.einsum(
        "kj,pjl->pkl", signed, last_imag, precision=highest
    )
    first_imag = jnp.einsum("kj,pjl->pkl", cosines, last_imag, precision=highest) + jnp.einsum(
        "kj,pjl->pkl", signed, last_real, precision=highest
    )
    return (first_real, first_imag)


def propagate(real_part, imag_part, tables, kernel_real, kernel_imag):
    spec_real, spec_imag = fourier_pair(real_part, imag_part, tables, -1.0)
    moved_real = spec_real * kernel_real - spec_imag * kernel_imag
    moved_imag = spec_real * kernel_imag + spec_imag * kernel_real
    return fourier_pair(moved_real, moved_imag, tables, 1.0)


def gradient_windows(windows, chosen, measured, tables, kernel_real, kernel_imag):
    wave_real, wave_imag = (chosen[:, 0], chosen[:, 1])
    entering = []
    for s in range(SLICES):
        if s > 0:
            wave_real, wave_imag = propagate(wave_real, wave_imag, tables, kernel_real, kernel_imag)
        entering.append((wave_real, wave_imag))
        slab_real, slab_imag = (windows[:, s, 0], windows[:, s, 1])
        wave_real, wave_imag = (
            wave_real * slab_real - wave_imag * slab_imag,
            wave_real * slab_imag + wave_imag * slab_real,
        )
    far_real, far_imag = fourier_pair(wave_real, wave_imag, tables, -1.0)
    residual = far_real * far_real + far_imag * far_imag - measured
    back_real, back_imag = fourier_pair(residual * far_real, residual * far_imag, tables, 1.0)
    pieces = [None] * SLICES
    for s in reversed(range(SLICES)):
        in_real, in_imag = entering[s]
        pieces[s] = jnp.stack(
            [in_real * back_real + in_imag * back_imag, in_real * back_imag - in_imag * back_real],
            axis=1,
        )
        slab_real, slab_imag = (windows[:, s, 0], windows[:, s, 1])
        back_real, back_imag = (
            slab_real * back_real + slab_imag * back_imag,
            slab_real * back_imag - slab_imag * back_real,
        )
        if s > 0:
            back_real, back_imag = propagate(
                back_real, back_imag, tables, kernel_real, -kernel_imag
            )
    return jnp.stack(pieces, axis=1)


def on_device(objects, probes, x_offsets, y_offsets, modes, measured):
    anchor = jnp.zeros((), jnp.int32)
    amount = x_offsets.shape[0]
    tables = fourier_tables(W)
    phase_map = kernel_phase(W)
    kernel_real = jnp.cos(phase_map)
    kernel_imag = -jnp.sin(phase_map)
    selector = modes[:, None] == jnp.arange(NPROBE, dtype=jnp.int32)[None, :]
    chosen = jnp.sum(jnp.where(selector[:, :, None, None, None], probes[None], 0.0), axis=1)
    neighbour = from_behind(objects, "lat", -1)
    extended = jnp.concatenate([objects, neighbour], axis=2)

    def fetch(x_offset, y_offset):
        return lax.dynamic_slice(extended, (anchor, anchor, x_offset, y_offset), (SLICES, 2, W, W))

    windows = jax.vmap(fetch)(x_offsets, y_offsets)
    pieces = gradient_windows(windows, chosen, measured, tables, kernel_real, kernel_imag)

    def add_window(i, buffer):
        corner = (anchor, anchor, x_offsets[i], y_offsets[i])
        current = lax.dynamic_slice(buffer, corner, (SLICES, 2, W, W))
        return lax.dynamic_update_slice(buffer, current + pieces[i], corner)

    buffer = lax.fori_loop(0, amount, add_window, jnp.zeros_like(extended))
    returned = from_behind(buffer[:, :, TILE:], "lat", 1)
    gradient = buffer[:, :, :TILE] + returned
    return objects - descent_rate * gradient


def solution(mesh):
    in_specs = (
        P(None, None, ("groups", "lat"), None),
        P("groups", None, None, None),
        P(("groups", "lat")),
        P(("groups", "lat")),
        P(("groups", "lat")),
        P(("groups", "lat"), None, None),
    )
    out_specs = P(None, None, ("groups", "lat"), None)
    return jax.shard_map(
        on_device, mesh=mesh, in_specs=in_specs, out_specs=out_specs, check_vma=False
    )
```

profile of v0, /device:TPU:16, one launch (start us, length us, event | category | flops | bytes accessed | tf_op | source)
XLA Modules:
  0.0 267.4 jit_solution(11585928870141830070)
XLA Ops:
  0.0 2.7 %collective-permute-start = (f32[2,2,256,1024]{3,2,1,0:T(8,128)}, f32[2,2,256,1024]{3,2,1,0:T(8,128)}, u32[]{:S(2)}, u32[]{:S(2)}) collective-permute-start(f32[2,2,256,1024]{3,2,1,0:T(8,128)} %param.8), channel_id=1, source_target_pairs={{1,0},{2,1},{3,2},{4,3},{5,4},{6,5},{7,6},{8,7},{9,8},{10,9},{11,1... | collective-permute-start | bytes 12582920 | tf_op jit(solution)/shard_map/ppermute | solution.py:22
  11.1 38.0 %collective-permute-done = f32[2,2,256,1024]{3,2,1,0:T(8,128)} collective-permute-done((f32[2,2,256,1024]{3,2,1,0:T(8,128)}, f32[2,2,256,1024]{3,2,1,0:T(8,128)}, u32[]{:S(2)}, u32[]{:S(2)}) %collective-permute-start) | collective-permute-done | bytes 4194336 | tf_op jit(solution)/shard_map/ppermute | solution.py:22
  49.1 8.3 %pad_maximum_fusion = f32[2,2,512,1024]{3,2,1,0:T(8,128)} fusion(f32[2,2,256,1024]{3,2,1,0:T(8,128)} %collective-permute-done, f32[2,2,256,1024]{3,2,1,0:T(8,128)} %param.8), kind=kLoop, calls=%fused_computation.5 | loop fusion | flops 2097152 | bytes 16777216 | tf_op jit(solution)/shard_map/concatenate | solution.py:108
  57.4 10.4 %while.15 = (s32[]{:T(128)}, f32[2,2,512,1024]{3,2,1,0:T(8,128)}, s32[2,4]{1,0:T(2,128)S(1)}, f32[2,2,2,256,256]{3,4,0,2,1:T(8,128)}, s32[]{:T(128)}) while((s32[]{:T(128)}, f32[2,2,512,1024]{3,2,1,0:T(8,128)}, s32[2,4]{1,0:T(2,128)S(1)}, f32[2,2,2,256,256]{3,4,0,2,1:T(8,128)}, s32[]{:T(128)}) %tuple.56), condition=%wide.while_cond, body=%wide.while_body.sunk | while | flops 2 | bytes 6291589 | solution.py:111
  58.0 3.0 %dynamic-slice_bitcast_fusion.2 = f32[1,2,2,256,256]{4,3,2,1,0:T(8,128)S(1)} fusion(f32[2,2,512,1024]{3,2,1,0:T(8,128)} %get-tuple-element.229, s32[]{:T(128)} %bitcast.265, s32[]{:T(128)} %bitcast.266), kind=kLoop, calls=%fused_computation.2.clone.1 | loop fusion | bytes 2097160 | tf_op jit(solution)/shard_map/vmap()/gather
  63.0 3.0 %dynamic-slice_bitcast_fusion.2 = f32[1,2,2,256,256]{4,3,2,1,0:T(8,128)S(1)} fusion(f32[2,2,512,1024]{3,2,1,0:T(8,128)} %get-tuple-element.229, s32[]{:T(128)} %bitcast.265, s32[]{:T(128)} %bitcast.266), kind=kLoop, calls=%fused_computation.2.clone.1 | loop fusion | bytes 2097160 | tf_op jit(solution)/shard_map/vmap()/gather
  80.5 2.0 fusion.10
  91.9 2.1 convolution_subtract_fusion.9
  103.2 2.2 convolution_add_fusion.7
  114.6 1.9 fusion.69
  116.5 2.1 fusion.73
  118.6 1.9 convolution_add_fusion.5
  122.3 1.9 convolution_subtract_fusion.5
  128.0 2.2 fusion.14
  139.5 2.3 fusion.63
  153.0 2.1 convolution_subtract_fusion.1
  162.2 4.3 %broadcast_in_dim.26 = f32[2,2,512,1024]{3,2,1,0:T(8,128)} broadcast(f32[]{:T(128)} %constant.73.clone.1), dimensions={} | broadcast | bytes 8388612 | tf_op jit(solution)/shard_map/broadcast_in_dim | solution.py:121
  166.5 40.8 %while.14 = (s32[]{:T(128)}, f32[2,2,512,1024]{3,2,1,0:T(8,128)}, s32[2]{0:T(128)S(1)}, s32[2]{0:T(128)S(1)}, f32[2,2,2,256,256]{3,4,0,2,1:T(8,128)}, /*index=5*/s32[]{:T(128)}, s32[]{:T(128)}, s32[]{:T(128)}, s32[]{:T(128)}) while((s32[]{:T(128)}, f32[2,2,512,1024]{3,2,1,0:T(8,128)}, s32[2]{0:T(128)S(1)}, s32[2]{0:T(128)S(1)}, ...), condition=%wide.region_2.3_spmd, body=%wide.region_1.2_spmd.sunk | while | flops 262152 | bytes 9437393 | solution.py:121
  174.9 11.9 %dynamic_update_slice.8 = f32[2,2,512,1024]{3,2,1,0:T(8,128)} dynamic-update-slice(f32[2,2,512,1024]{3,2,1,0:T(8,128)} %get-tuple-element.243, f32[2,2,256,256]{3,2,1,0:T(8,128)S(1)} %bitcast_add_fusion.2, s32[]{:T(128)} %constant.72.clone.1..sunk, s32[]{:T(128)} %constant.72.clone.1..sunk, s32[]{:T(128)S(6)} %select_n.348, s32[]{:T(128)S(6)} %select_n.349) | dynamic-update-slice | bytes 2097156 | tf_op jit(solution)/shard_map/while/body/eval_jaxpr/dynamic_update_slice | solution.py:119
  195.2 12.1 %dynamic_update_slice.8 = f32[2,2,512,1024]{3,2,1,0:T(8,128)} dynamic-update-slice(f32[2,2,512,1024]{3,2,1,0:T(8,128)} %get-tuple-element.243, f32[2,2,256,256]{3,2,1,0:T(8,128)S(1)} %bitcast_add_fusion.2, s32[]{:T(128)} %constant.72.clone.1..sunk, s32[]{:T(128)} %constant.72.clone.1..sunk, s32[]{:T(128)S(6)} %select_n.348, s32[]{:T(128)S(6)} %select_n.349) | dynamic-update-slice | bytes 2097156 | tf_op jit(solution)/shard_map/while/body/eval_jaxpr/dynamic_update_slice | solution.py:119
  207.3 2.7 slice.33
  210.0 3.2 %collective-permute-start.1 = (f32[2,2,256,1024]{3,2,1,0:T(8,128)S(1)}, f32[2,2,256,1024]{3,2,1,0:T(8,128)S(1)}, u32[]{:S(2)}, u32[]{:S(2)}) collective-permute-start(f32[2,2,256,1024]{3,2,1,0:T(8,128)S(1)} %slice.33), channel_id=1, source_target_pairs={{0,1},{1,2},{2,3},{3,4},{4,5},{5,6},{6,7},{7,8},{8,9},{9,10},{10,1... | collective-permute-start | bytes 12582920 | tf_op jit(solution)/shard_map/ppermute | solution.py:22
  213.2 48.3 %collective-permute-done.1 = f32[2,2,256,1024]{3,2,1,0:T(8,128)S(1)} collective-permute-done((f32[2,2,256,1024]{3,2,1,0:T(8,128)S(1)}, f32[2,2,256,1024]{3,2,1,0:T(8,128)S(1)}, u32[]{:S(2)}, u32[]{:S(2)}) %collective-permute-start.1) | collective-permute-done | bytes 4194336 | tf_op jit(solution)/shard_map/ppermute | solution.py:22
  261.5 5.7 %add_subtract_fusion = f32[2,2,256,1024]{3,2,1,0:T(8,128)} fusion(f32[2,2,256,1024]{3,2,1,0:T(8,128)} %param.8, f32[2,2,256,1024]{3,2,1,0:T(8,128)S(1)} %collective-permute-done.1, f32[2,2,512,1024]{3,2,1,0:T(8,128)S(1)} %copy-done), kind=kLoop, calls=%fused_computation.6 | loop fusion | flops 2097152 | bytes 16777216 | tf_op jit(solution)/shard_map/sub | solution.py:124
  (87 shorter events, 94.8 us)
Async XLA Ops:
  0.0 49.1 %collective-permute-start = (f32[2,2,256,1024]{3,2,1,0:T(8,128)}, f32[2,2,256,1024]{3,2,1,0:T(8,128)}, u32[]{:S(2)}, u32[]{:S(2)}) collective-permute-start(f32[2,2,256,1024]{3,2,1,0:T(8,128)} %param.8), channel_id=1, source_target_pairs={{1,0},{2,1},{3,2},{4,3},{5,4},{6,5},{7,6},{8,7},{9,8},{10,9},{11,1... | collective-permute-start | bytes 12582920 | tf_op jit(solution)/shard_map/ppermute | solution.py:22
  88.1 9.5 %copy-start.3 = (f32[2,2,2,256,256]{3,4,0,2,1:T(8,128)S(1)}, f32[2,2,2,256,256]{3,4,0,2,1:T(8,128)}, u32[]{:S(2)}) copy-start(f32[2,2,2,256,256]{3,4,0,2,1:T(8,128)} %get-tuple-element.107) | copy-start | bytes 6291460
  149.2 9.4 %copy-start.1 = (f32[2,1,256,256]{2,3,0,1:T(8,128)S(1)}, f32[2,1,256,256]{2,3,0,1:T(8,128)}, u32[]{:S(2)}) copy-start(f32[2,1,256,256]{2,3,0,1:T(8,128)} %copy.172) | copy-start | bytes 1572868
  149.2 9.4 %copy-start.2 = (f32[2,1,256,256]{2,3,0,1:T(8,128)S(1)}, f32[2,1,256,256]{2,3,0,1:T(8,128)}, u32[]{:S(2)}) copy-start(f32[2,1,256,256]{2,3,0,1:T(8,128)} %copy.173) | copy-start | bytes 1572868
  162.2 4.3 %copy-start.4 = (s32[2]{0:T(128)S(1)}, s32[2]{0:T(128)}, u32[]{:S(2)}) copy-start(s32[2]{0:T(128)} %param.10) | copy-start | bytes 28
  162.2 4.3 %copy-start.5 = (s32[2]{0:T(128)S(1)}, s32[2]{0:T(128)}, u32[]{:S(2)}) copy-start(s32[2]{0:T(128)} %param.11) | copy-start | bytes 28
  207.3 54.2 %copy-start = (f32[2,2,512,1024]{3,2,1,0:T(8,128)S(1)}, f32[2,2,512,1024]{3,2,1,0:T(8,128)}, u32[]{:S(2)}) copy-start(f32[2,2,512,1024]{3,2,1,0:T(8,128)} %get-tuple-element.99) | copy-start | bytes 25165828
  210.0 51.5 %collective-permute-start.1 = (f32[2,2,256,1024]{3,2,1,0:T(8,128)S(1)}, f32[2,2,256,1024]{3,2,1,0:T(8,128)S(1)}, u32[]{:S(2)}, u32[]{:S(2)}) collective-permute-start(f32[2,2,256,1024]{3,2,1,0:T(8,128)S(1)} %slice.33), channel_id=1, source_target_pairs={{0,1},{1,2},{2,3},{3,4},{4,5},{5,6},{6,7},{7,8},{8,9},{9,10},{10,1... | collective-permute-start | bytes 12582920 | tf_op jit(solution)/shard_map/ppermute | solution.py:22
where the time goes:
time: 272 us; the launch traced here: 267 us
  matrix products  90.6 us (33%)
  waiting for transfers between devices  86.3 us (32%)
  local copies, waits for them, and re-layouts  50.1 us (18%)
  other arithmetic  25.8 us (9%)
  loops' own time  7.97 us (3%)
  starting transfers between devices  5.95 us (2%)
    ppermute x2, waiting for transfers between devices, from_behind(): return lax.ppermute(block, axis, route)  86.3 us
    dynamic_update_slice x2, local copies, waits for them, and re-layouts, add_window(): return lax.dynamic_update_slice(buffer, current + pieces[i], corner)  24 us
    dot_general x6, matrix products, fourier_pair(): jnp.einsum('pjk,kl->pjl', real_part, signed, precision=highest)  11.6 us
    dot_general x6, matrix products, fourier_pair(): jnp.einsum('pjk,kl->pjl', imag_part, signed, precision=highest)  11.6 us
    dot_general x6, matrix products, fourier_pair(): jnp.einsum('kj,pjl->pkl', signed, last_imag, precision=highest)  11.5 us
    dot_general x6, matrix products, fourier_pair(): jnp.einsum('kj,pjl->pkl', cosines, last_real, precision=highest)  11.4 us
    dot_general x6, matrix products, fourier_pair(): jnp.einsum('pjk,kl->pjl', real_part, cosines, precision=highest)  11.3 us
    dot_general x6, matrix products, fourier_pair(): jnp.einsum('pjk,kl->pjl', imag_part, cosines, precision=highest)  11.1 us
  transfers between devices with their start and end apart: 2, of which 2 were waited for; matrix products, arithmetic and copies ran while one was open for 3% of the time, Pallas kernels for 0%

commit v1 on v0

v1 whole, which is shorter than its diff:
```python
import functools
import math

import jax
import jax.numpy as jnp
import numpy as np
from jax import lax
from jax.experimental import pallas as pl
from jax.experimental.pallas import tpu as pltpu
from jax.sharding import PartitionSpec as P

SPREAD_PHASE = 40.0
LANES = 128


def permute_along(block, axis, distance):
    devices = range(lax.axis_size(axis))
    route = [(i - distance, i) for i in devices if i - distance in devices]
    return lax.ppermute(block, axis, route)


def matrix_tables(width):
    counter = np.arange(width)
    angles = (counter[:, None] * counter[None, :] % width) * (2.0 * math.pi / width)
    wave = np.exp(1j * angles) / math.sqrt(width)
    folded = ((counter + width // 2) % width - width // 2) / width
    phases = np.exp(-1j * SPREAD_PHASE * folded**2)
    spread = (wave * phases[None, :]) @ np.conj(wave)
    spread = (spread + spread.T) / 2
    stacked = np.stack([spread.real, spread.imag, wave.real, wave.imag])
    high = stacked.astype(jnp.bfloat16)
    low = (stacked - high.astype(np.float64)).astype(jnp.bfloat16)
    return high, low


def split(value):
    high = value.astype(jnp.bfloat16)
    return high, (value - high.astype(jnp.float32)).astype(jnp.bfloat16)


def pack_kernel(scalars, a_ref, b_ref, c_ref, out_ref):
    shift = scalars[1]
    wide = jnp.concatenate([a_ref[0, 0], b_ref[0, 0], c_ref[0, 0]], axis=1)
    width = wide.shape[1]
    out_ref[0, 0] = pltpu.roll(wide, width - shift, 1)[:, : out_ref.shape[3]]


def pack_windows(objects, columns, window):
    slices, parts, tile, _ = objects.shape

    def block(j):
        return pl.BlockSpec(
            (1, 1, tile, LANES), lambda i, s: (i // parts, i % parts, 0, s[0] + j)
        )

    return pl.pallas_call(
        pack_kernel,
        grid_spec=pltpu.PrefetchScalarGridSpec(
            num_scalar_prefetch=1,
            grid=(slices * parts,),
            in_specs=[block(0), block(1), block(2)],
            out_specs=pl.BlockSpec((1, 1, tile, window), lambda i, s: (i // parts, i % parts, 0, 0)),
        ),
        out_shape=jax.ShapeDtypeStruct((slices, parts, tile, window), jnp.float32),
        cost_estimate=pl.CostEstimate(flops=10**6, bytes_accessed=10 * 2**18, transcendentals=0),
        name="pack",
    )(columns, objects, objects, objects)


def cmul(ar, ai, br, bi):
    return ar * br - ai * bi, ar * bi + ai * br


def cmul_conj(ar, ai, br, bi):
    return ar * br + ai * bi, ar * bi - ai * br


def window_kernel(scalars, a_ref, b_ref, c_ref, recv_ref, probe_ref, measured_ref,
                  col_high, col_low, row_high, row_low, own_ref, ret_ref,
                  extended, win, left_high, left_low, right_high, right_low, entry, field):
    shift, rows = scalars[1], scalars[2]
    slices, parts, tile, window = recv_ref.shape
    offset = lax.rem(rows, 8)
    base = pl.multiple_of(rows - offset, 8)
    padded = window + 8

    for s in range(slices):
        for c in range(parts):
            wide = jnp.concatenate([a_ref[s, c], b_ref[s, c], c_ref[s, c]], axis=1)
            extended[0:tile] = pltpu.roll(wide, wide.shape[1] - shift, 1)[:, :window]
            extended[tile : 2 * tile] = recv_ref[s, c]
            loaded = extended[pl.ds(base, padded), :]
            win[s, c] = pltpu.roll(loaded, padded - offset, 0)[:window]

    def transform(real, imag, table, sign):
        high, low = split(real)
        left_high[0:window, 0:window] = high
        left_low[0:window, 0:window] = low
        left_high[window:, window:] = high * sign
        left_low[window:, window:] = low * sign
        high, low = split(imag)
        left_high[window:, 0:window] = high
        left_low[window:, 0:window] = low
        left_high[0:window, window:] = high * -sign
        left_low[0:window, window:] = low * -sign
        product = functools.partial(jnp.dot, preferred_element_type=jnp.float32)
        last = (product(left_high[...], col_high[table]) + product(left_high[...], col_low[table])
                + product(left_low[...], col_high[table]))
        high, low = split(last[0:window])
        right_high[0:window, 0:window] = high
        right_low[0:window, 0:window] = low
        right_high[window:, window:] = high * sign
        right_low[window:, window:] = low * sign
        high, low = split(last[window:])
        right_high[0:window, window:] = high
        right_low[0:window, window:] = low
        right_high[window:, 0:window] = high * -sign
        right_low[window:, 0:window] = low * -sign
        first = (product(row_high[table], right_high[...]) + product(row_high[table], right_low[...])
                 + product(row_low[table], right_high[...]))
        return first[:, 0:window], first[:, window:]

    def store_piece(s, piece):
        for c in range(parts):
            value = jnp.concatenate([piece[c], jnp.zeros((8, window), jnp.float32)], axis=0)
            extended[...] = jnp.zeros_like(extended)
            extended[pl.ds(base, padded), :] = pltpu.roll(value, offset, 0)
            own_ref[s, c] = extended[0:tile]
            ret_ref[s, c] = extended[tile : 2 * tile]

    one = jnp.bfloat16(1)
    er, ei = transform(*cmul(probe_ref[0, 0], probe_ref[0, 1], win[0, 0], win[0, 1]), 0, one)
    entry[0] = er
    entry[1] = ei
    fr, fi = transform(*cmul(entry[0], entry[1], win[1, 0], win[1, 1]), 1, -one)
    residual = fr * fr + fi * fi - measured_ref[0]
    gr, gi = transform(residual * fr, residual * fi, 1, one)
    field[0] = gr
    field[1] = gi
    store_piece(1, cmul_conj(entry[0], entry[1], field[0], field[1]))
    gr, gi = transform(*cmul_conj(win[1, 0], win[1, 1], field[0], field[1]), 0, -one)
    field[0] = gr
    field[1] = gi
    store_piece(0, cmul_conj(probe_ref[0, 0], probe_ref[0, 1], field[0], field[1]))


def window_gradient(objects, received, probes, measured, tables, scalars, position):
    slices, parts, tile, _ = objects.shape
    window = measured.shape[-1]
    shape = (slices, parts, tile, window)

    def block(j):
        return pl.BlockSpec((slices, parts, tile, LANES), lambda i, s: (0, 0, 0, s[0] + j))

    def whole(array):
        return pl.BlockSpec(array.shape, lambda i, s: (0,) * array.ndim)

    return pl.pallas_call(
        window_kernel,
        grid_spec=pltpu.PrefetchScalarGridSpec(
            num_scalar_prefetch=1,
            grid=(1,),
            in_specs=[
                block(0), block(1), block(2),
                whole(received),
                pl.BlockSpec((1, parts, window, window), lambda i, s: (s[3], 0, 0, 0)),
                pl.BlockSpec((1, window, window), lambda i, s: (position, 0, 0)),
                *[whole(t) for t in tables],
            ],
            out_specs=[pl.BlockSpec(shape, lambda i, s: (0, 0, 0, 0))] * 2,
            scratch_shapes=[
                pltpu.VMEM((2 * tile + 8, window), jnp.float32),
                pltpu.VMEM((slices, parts, window, window), jnp.float32),
                *[pltpu.VMEM((2 * window, 2 * window), jnp.bfloat16)] * 4,
                pltpu.VMEM((parts, window, window), jnp.float32),
                pltpu.VMEM((parts, window, window), jnp.float32),
            ],
        ),
        out_shape=[jax.ShapeDtypeStruct(shape, jnp.float32)] * 2,
        cost_estimate=pl.CostEstimate(flops=6 * 10**9, bytes_accessed=6 * 2**20, transcendentals=0),
        name="window_gradient",
    )(scalars, objects, objects, objects, received, probes, measured, *tables)


def final_kernel(scalars, objects_ref, *refs):
    piece_refs, out_ref = refs[:-1], refs[-1]
    out_ref[...] = objects_ref[...]
    for k, piece_ref in enumerate(piece_refs):
        start = pl.multiple_of(scalars[2 * k] * LANES, LANES)
        piece = piece_ref[0, 0]
        wide = jnp.concatenate([piece, jnp.zeros((piece.shape[0], LANES), jnp.float32)], axis=1)
        columns = pl.ds(start, wide.shape[1])
        out_ref[0, 0, :, columns] = out_ref[0, 0, :, columns] - pltpu.roll(wide, scalars[2 * k + 1], 1)


def subtract_pieces(objects, pieces, columns):
    slices, parts, tile, length = objects.shape
    index = lambda i, s: (i // parts, i % parts, 0, 0)
    return pl.pallas_call(
        final_kernel,
        grid_spec=pltpu.PrefetchScalarGridSpec(
            num_scalar_prefetch=1,
            grid=(slices * parts,),
            in_specs=[pl.BlockSpec((1, 1, tile, length), index)]
            + [pl.BlockSpec((1, 1) + piece.shape[2:], index) for piece in pieces],
            out_specs=pl.BlockSpec((1, 1, tile, length), index),
        ),
        out_shape=jax.ShapeDtypeStruct(objects.shape, jnp.float32),
        cost_estimate=pl.CostEstimate(flops=10**6, bytes_accessed=12 * 2**20, transcendentals=0),
        name="subtract",
    )(columns, objects, *pieces)


def on_device(objects, probes, x_offsets, y_offsets, modes, measured):
    amount, window = measured.shape[0], measured.shape[-1]
    length = objects.shape[-1]
    high, low = matrix_tables(window)
    columns = lambda t: jnp.asarray(np.concatenate([t[0::2], t[1::2]], axis=1))
    rows = lambda t: jnp.asarray(np.concatenate([t[0::2], t[1::2]], axis=2))
    tables = (columns(high), columns(low), rows(high), rows(low))

    def blocks_of(offsets):
        block = jnp.minimum(offsets // LANES, (length - window) // LANES - 1)
        return jnp.stack([block, offsets - block * LANES], axis=1)

    left_blocks = blocks_of(permute_along(y_offsets, "lat", 1))
    own_blocks = blocks_of(y_offsets)
    sent = [pack_windows(objects, left_blocks[p], window) for p in range(amount)]
    received = [permute_along(block, "lat", -1) for block in sent]
    own, returned = [], []
    for p in range(amount):
        scalars = jnp.concatenate([own_blocks[p], x_offsets[p : p + 1], modes[p : p + 1]])
        mine, theirs = window_gradient(objects, received[p], probes, measured, tables, scalars, p)
        own.append(mine)
        returned.append(permute_along(theirs, "lat", 1))
    where = jnp.concatenate([own_blocks.reshape(-1), left_blocks.reshape(-1)])
    return subtract_pieces(objects, own + returned, where)


def solution(mesh):
    in_specs = (
        P(None, None, ("groups", "lat"), None),
        P("groups", None, None, None),
        P(("groups", "lat")),
        P(("groups", "lat")),
        P(("groups", "lat")),
        P(("groups", "lat"), None, None),
    )
    out_specs = P(None, None, ("groups", "lat"), None)
    return jax.shard_map(
        on_device, mesh=mesh, in_specs=in_specs, out_specs=out_specs, check_vma=False
    )
```

time: 272 us -> 81.6 us (0.30); the launches traced: 267 us -> 80.8 us
  matrix products: 90.6 us -> 0 us
  waiting for transfers between devices: 86.3 us -> 19.2 us
  local copies, waits for them, and re-layouts: 50.1 us -> 4.84 us
  Pallas kernels: 0 us -> 41.4 us
  other arithmetic: 25.8 us -> 4.34 us
  loops' own time: 7.97 us -> 0 us
  starting transfers between devices: 5.95 us -> 10.9 us
    dot_general x48 -> x0, matrix products: 90.6 us -> none  [the longest x6 11.6 us: fourier_pair(): jnp.einsum('pjk,kl->pjl', real_part, signed, precision=highest)]
    ppermute x2 -> x5, waiting for transfers between devices: 86.3 us -> 19.2 us  [permute_along(): return lax.ppermute(block, axis, route)]
    pallas_call x0 -> x5, Pallas kernels: none -> 41.4 us  [the longest x2 24.9 us: window_gradient(): pl.pallas_call(window_kernel, grid_spec=pltpu.PrefetchScalarGridSpec(num_...]
    dynamic_update_slice x2 -> x0, local copies, waits for them, and re-layouts: 24 us -> none  [add_window(): return lax.dynamic_update_slice(buffer, current + pieces[i], corner)]
    gather x10 -> x0, local copies, waits for them, and re-layouts: 9.92 us -> none
    another operation x2 -> x0, loops' own time: 7.97 us -> none  [the longest x1 7.51 us: on_device(): buffer = lax.fori_loop(0, amount, add_window, jnp.zeros_like(extended))]
    sub x2 -> x0, other arithmetic: 7.4 us -> none  [the longest x1 5.73 us: on_device(): return objects - descent_rate * gradient]
    dynamic_slice x8 -> x0, local copies, waits for them, and re-layouts: 5.69 us -> none  [the longest x4 3.28 us: add_window(): return lax.dynamic_update_slice(buffer, current + pieces[i], corner)]
  transfers between devices with their start and end apart: 2 -> 5, of which waited for: 2 -> 3; matrix products, arithmetic and copies ran while one was open for 3% -> 7% of each run, Pallas kernels for 0% -> 37%
where the time goes in v1:
time: 81.6 us; the launch traced here: 80.8 us
  Pallas kernels  41.4 us (51%)
  waiting for transfers between devices  19.2 us (24%)
  starting transfers between devices  10.9 us (13%)
  local copies, waits for them, and re-layouts  4.84 us (6%)
  other arithmetic  4.34 us (5%)
    pallas_call x2, Pallas kernels, window_gradient(): pl.pallas_call(window_kernel, grid_spec=pltpu.PrefetchScalarGridSpec(num_...  24.9 us
    ppermute x5, waiting for transfers between devices, permute_along(): return lax.ppermute(block, axis, route)  19.2 us
    ppermute x5, starting transfers between devices, permute_along(): return lax.ppermute(block, axis, route)  10.9 us
    pallas_call x2, Pallas kernels, pack_windows(): pl.pallas_call(pack_kernel, grid_spec=pltpu.PrefetchScalarGridSpec(num_sc...  9.36 us
    pallas_call x1, Pallas kernels, subtract_pieces(): pl.pallas_call(final_kernel, grid_spec=pltpu.PrefetchScalarGridSpec(num_s...  7.19 us
    concatenate x2, other arithmetic, on_device(): jnp.concatenate([own_blocks[p], x_offsets[p:p + 1], modes[p:p + 1]])  3.68 us
    unnamed x14, local copies, waits for them, and re-layouts  2.94 us
  transfers between devices with their start and end apart: 5, of which 3 were waited for; matrix products, arithmetic and copies ran while one was open for 7% of the time, Pallas kernels for 37%

profile of v1, /device:TPU:16, one launch (start us, length us, event | category | flops | bytes accessed | tf_op | source)
XLA Modules:
  0.0 80.8 jit_solution(7400817532557724927)
XLA Ops:
  0.0 1.9 %collective-permute-start = (s32[2]{0:T(128)}, s32[2]{0:T(128)S(1)}, u32[]{:S(2)}, u32[]{:S(2)}) collective-permute-start(s32[2]{0:T(128)} %param.13), channel_id=1, source_target_pairs={{0,1},{1,2},{2,3},{3,4},{4,5},{5,6},{6,7},{7,8},{8,9},{9,10},{10,1... | collective-permute-start | bytes 32 | tf_op jit(solution)/shard_map/ppermute | solution.py:19
  1.9 4.0 %collective-permute-done = s32[2]{0:T(128)S(1)} collective-permute-done((s32[2]{0:T(128)}, s32[2]{0:T(128)S(1)}, u32[]{:S(2)}, u32[]{:S(2)}) %collective-permute-start) | collective-permute-done | bytes 40 | tf_op jit(solution)/shard_map/ppermute | solution.py:19
  5.9 0.8 slice_reduce_fusion
  6.7 4.7 %pack.2 = f32[2,2,256,256]{3,2,1,0:T(8,128)} custom-call(s32[2]{0:T(128)} %get-tuple-element.14.scalars, f32[2,2,256,1024]{3,2,1,0:T(8,128)} %objects_ref.1, f32[2,2,256,1024]{3,2,1,0:T(8,128)} %objects_ref.1, f32[2,2,256,1024]{3,2,1,0:T(8,128)} %objects_ref.1), custom_call_target="tpu_custom_call" | custom-call | flops 1000000 | bytes 2621440 | tf_op jit(solution)/shard_map/pack/pallas_call | solution.py:56
  11.4 1.9 %collective-permute-start.1 = (f32[2,2,256,256]{3,2,1,0:T(8,128)}, f32[2,2,256,256]{3,2,1,0:T(8,128)S(1)}, u32[]{:S(2)}, u32[]{:S(2)}) collective-permute-start(f32[2,2,256,256]{3,2,1,0:T(8,128)} %pack.2), channel_id=1, source_target_pairs={{1,0},{2,1},{3,2},{4,3},{5,4},{6,5},{7,6},{8,7},{9,8},{10,9},{11,1... | collective-permute-start | bytes 3145736 | tf_op jit(solution)/shard_map/ppermute | solution.py:19
  13.3 4.7 %pack.3 = f32[2,2,256,256]{3,2,1,0:T(8,128)} custom-call(s32[2]{0:T(128)} %get-tuple-element.13.scalars, f32[2,2,256,1024]{3,2,1,0:T(8,128)} %objects_ref.1, f32[2,2,256,1024]{3,2,1,0:T(8,128)} %objects_ref.1, f32[2,2,256,1024]{3,2,1,0:T(8,128)} %objects_ref.1), custom_call_target="tpu_custom_call" | custom-call | flops 1000000 | bytes 2621440 | tf_op jit(solution)/shard_map/pack/pallas_call | solution.py:56
  18.0 2.5 %collective-permute-start.2 = (f32[2,2,256,256]{3,2,1,0:T(8,128)}, f32[2,2,256,256]{3,2,1,0:T(8,128)S(1)}, u32[]{:S(2)}, u32[]{:S(2)}) collective-permute-start(f32[2,2,256,256]{3,2,1,0:T(8,128)} %pack.3), channel_id=1, source_target_pairs={{1,0},{2,1},{3,2},{4,3},{5,4},{6,5},{7,6},{8,7},{9,8},{10,9},{11,1... | collective-permute-start | bytes 3145736 | tf_op jit(solution)/shard_map/ppermute | solution.py:19
  20.6 0.2 slice_reduce_fusion.1
  20.8 0.6 fusion.4
  21.4 1.9 %pad_add_fusion.4.scalars = s32[4]{0:T(128)} fusion(s32[1]{0:T(128)} %get-tuple-element.26, s32[1]{0:T(128)} %get-tuple-element.21, s32[2]{0:T(128)S(1)} %get-tuple-element.15), kind=kLoop, calls=%fused_computation.16 | loop fusion | flops 8 | bytes 32 | tf_op jit(solution)/shard_map/concatenate | solution.py:232
  23.2 1.8 %pad_add_fusion.3.scalars = s32[4]{0:T(128)} fusion(s32[1]{0:T(128)} %get-tuple-element.25, s32[1]{0:T(128)} %get-tuple-element.22, s32[2]{0:T(128)S(1)} %get-tuple-element.16), kind=kLoop, calls=%fused_computation.15 | loop fusion | flops 8 | bytes 32 | tf_op jit(solution)/shard_map/concatenate | solution.py:232
  25.0 0.9 %collective-permute-done.1.recv_ref = f32[2,2,256,256]{3,2,1,0:T(8,128)S(1)} collective-permute-done((f32[2,2,256,256]{3,2,1,0:T(8,128)}, f32[2,2,256,256]{3,2,1,0:T(8,128)S(1)}, u32[]{:S(2)}, u32[]{:S(2)}) %collective-permute-start.1) | collective-permute-done | bytes 1048608 | tf_op jit(solution)/shard_map/ppermute | solution.py:19
  25.9 1.0 %copy-done.5 = f32[2,2,256,256]{3,2,1,0:T(8,128)} copy-done((f32[2,2,256,256]{3,2,1,0:T(8,128)}, f32[2,2,256,256]{3,2,1,0:T(8,128)S(1)}, u32[]{:S(2)}) %copy-start.5) | copy-done | bytes 1048600
  26.9 12.5 %window_gradient.2 = (f32[2,2,256,256]{3,2,1,0:T(8,128)}, f32[2,2,256,256]{3,2,1,0:T(8,128)}) custom-call(s32[4]{0:T(128)} %pad_add_fusion.3.scalars, f32[2,2,256,1024]{3,2,1,0:T(8,128)} %objects_ref.1, f32[2,2,256,1024]{3,2,1,0:T(8,128)} %objects_ref.1, f32[2,2,256,1024]{3,2,1,0:T(8,128)} %objects_ref.1, f32[2,2,256,256]{3,2,1,0:T(8,128)} %copy-done.5, ...), custom_call_target="tpu_custom_call" | custom-call | flops 6000000000 | bytes 6291456 | tf_op jit(solution)/shard_map/window_gradient/pallas_call | solution.py:158
  39.3 2.7 %collective-permute-start.3 = (f32[2,2,256,256]{3,2,1,0:T(8,128)}, f32[2,2,256,256]{3,2,1,0:T(8,128)S(1)}, u32[]{:S(2)}, u32[]{:S(2)}) collective-permute-start(f32[2,2,256,256]{3,2,1,0:T(8,128)} %get-tuple-element.11), channel_id=1, source_target_pairs={{0,1},{1,2},{2,3},{3,4},{4,5},{5,6},{6,7},{7,8},{8,9},{9,10},{10,1... | collective-permute-start | bytes 3145736 | tf_op jit(solution)/shard_map/ppermute | solution.py:19
  42.1 1.0 %copy-done.4 = f32[2,2,256,256]{3,2,1,0:T(8,128)} copy-done((f32[2,2,256,256]{3,2,1,0:T(8,128)}, f32[2,2,256,256]{3,2,1,0:T(8,128)S(1)}, u32[]{:S(2)}) %copy-start.4) | copy-done | bytes 1048600
  43.0 12.4 %window_gradient.3 = (f32[2,2,256,256]{3,2,1,0:T(8,128)}, f32[2,2,256,256]{3,2,1,0:T(8,128)}) custom-call(s32[4]{0:T(128)} %pad_add_fusion.4.scalars, f32[2,2,256,1024]{3,2,1,0:T(8,128)} %objects_ref.1, f32[2,2,256,1024]{3,2,1,0:T(8,128)} %objects_ref.1, f32[2,2,256,1024]{3,2,1,0:T(8,128)} %objects_ref.1, f32[2,2,256,256]{3,2,1,0:T(8,128)} %copy-done.4, ...), custom_call_target="tpu_custom_call" | custom-call | flops 6000000000 | bytes 6291456 | tf_op jit(solution)/shard_map/window_gradient/pallas_call | solution.py:158
  55.4 1.9 %collective-permute-start.4 = (f32[2,2,256,256]{3,2,1,0:T(8,128)}, f32[2,2,256,256]{3,2,1,0:T(8,128)S(1)}, u32[]{:S(2)}, u32[]{:S(2)}) collective-permute-start(f32[2,2,256,256]{3,2,1,0:T(8,128)} %get-tuple-element.12), channel_id=1, source_target_pairs={{0,1},{1,2},{2,3},{3,4},{4,5},{5,6},{6,7},{7,8},{8,9},{9,10},{10,1... | collective-permute-start | bytes 3145736 | tf_op jit(solution)/shard_map/ppermute | solution.py:19
  57.3 0.1 copy.13
  57.5 0.1 copy.14
  57.7 0.6 pad_add_fusion.2.scalars
  58.3 14.3 %collective-permute-done.4.refs_3_ = f32[2,2,256,256]{3,2,1,0:T(8,128)S(1)} collective-permute-done((f32[2,2,256,256]{3,2,1,0:T(8,128)}, f32[2,2,256,256]{3,2,1,0:T(8,128)S(1)}, u32[]{:S(2)}, u32[]{:S(2)}) %collective-permute-start.4) | collective-permute-done | bytes 1048608 | tf_op jit(solution)/shard_map/ppermute | solution.py:19
  72.7 1.0 %copy-done.1 = f32[2,2,256,256]{3,2,1,0:T(8,128)} copy-done((f32[2,2,256,256]{3,2,1,0:T(8,128)}, f32[2,2,256,256]{3,2,1,0:T(8,128)S(1)}, u32[]{:S(2)}) %copy-start.1) | copy-done | bytes 1048600
  73.6 7.2 %subtract.1 = f32[2,2,256,1024]{3,2,1,0:T(8,128)} custom-call(s32[8]{0:T(128)} %pad_add_fusion.2.scalars, f32[2,2,256,1024]{3,2,1,0:T(8,128)} %objects_ref.1, f32[2,2,256,256]{3,2,1,0:T(8,128)} %get-tuple-element.9.refs_0_, f32[2,2,256,256]{3,2,1,0:T(8,128)} %get-tuple-element.10.refs_1_, f32[2,2,256,256]{3,2,1,0:T(8,128)} %copy-done, ...), custom_call_target="tpu_custom_call" | custom-call | flops 1000000 | bytes 12582912 | tf_op jit(solution)/shard_map/subtract/pallas_call | solution.py:199
  (19 shorter events, 0.2 us)
Async XLA Ops:
  0.0 5.9 %collective-permute-start = (s32[2]{0:T(128)}, s32[2]{0:T(128)S(1)}, u32[]{:S(2)}, u32[]{:S(2)}) collective-permute-start(s32[2]{0:T(128)} %param.13), channel_id=1, source_target_pairs={{0,1},{1,2},{2,3},{3,4},{4,5},{5,6},{6,7},{7,8},{8,9},{9,10},{10,1... | collective-permute-start | bytes 32 | tf_op jit(solution)/shard_map/ppermute | solution.py:19
  6.7 6.6 %copy-start.6 = (s32[2]{0:T(128)S(1)}, s32[2]{0:T(128)}, u32[]{:S(2)}) copy-start(s32[2]{0:T(128)} %param.13) | copy-start | bytes 28
  11.4 14.5 %collective-permute-start.1 = (f32[2,2,256,256]{3,2,1,0:T(8,128)}, f32[2,2,256,256]{3,2,1,0:T(8,128)S(1)}, u32[]{:S(2)}, u32[]{:S(2)}) collective-permute-start(f32[2,2,256,256]{3,2,1,0:T(8,128)} %pack.2), channel_id=1, source_target_pairs={{1,0},{2,1},{3,2},{4,3},{5,4},{6,5},{7,6},{8,7},{9,8},{10,9},{11,1... | collective-permute-start | bytes 3145736 | tf_op jit(solution)/shard_map/ppermute | solution.py:19
  13.3 7.4 %copy-start.2 = (s32[2]{0:T(128)S(1)}, s32[2]{0:T(128)}, u32[]{:S(2)}) copy-start(s32[2]{0:T(128)} %param.12) | copy-start | bytes 28
  13.3 7.4 %copy-start.3 = (s32[2]{0:T(128)S(1)}, s32[2]{0:T(128)}, u32[]{:S(2)}) copy-start(s32[2]{0:T(128)} %param.14) | copy-start | bytes 28
  18.0 24.0 %collective-permute-start.2 = (f32[2,2,256,256]{3,2,1,0:T(8,128)}, f32[2,2,256,256]{3,2,1,0:T(8,128)S(1)}, u32[]{:S(2)}, u32[]{:S(2)}) collective-permute-start(f32[2,2,256,256]{3,2,1,0:T(8,128)} %pack.3), channel_id=1, source_target_pairs={{1,0},{2,1},{3,2},{4,3},{5,4},{6,5},{7,6},{8,7},{9,8},{10,9},{11,1... | collective-permute-start | bytes 3145736 | tf_op jit(solution)/shard_map/ppermute | solution.py:19
  25.9 1.0 %copy-start.5 = (f32[2,2,256,256]{3,2,1,0:T(8,128)}, f32[2,2,256,256]{3,2,1,0:T(8,128)S(1)}, u32[]{:S(2)}) copy-start(f32[2,2,256,256]{3,2,1,0:T(8,128)S(1)} %collective-permute-done.1.recv_ref) | copy-start | bytes 3145732
  39.3 19.0 %collective-permute-start.3 = (f32[2,2,256,256]{3,2,1,0:T(8,128)}, f32[2,2,256,256]{3,2,1,0:T(8,128)S(1)}, u32[]{:S(2)}, u32[]{:S(2)}) collective-permute-start(f32[2,2,256,256]{3,2,1,0:T(8,128)} %get-tuple-element.11), channel_id=1, source_target_pairs={{0,1},{1,2},{2,3},{3,4},{4,5},{5,6},{6,7},{7,8},{8,9},{9,10},{10,1... | collective-permute-start | bytes 3145736 | tf_op jit(solution)/shard_map/ppermute | solution.py:19
  42.0 1.0 %copy-start.4 = (f32[2,2,256,256]{3,2,1,0:T(8,128)}, f32[2,2,256,256]{3,2,1,0:T(8,128)S(1)}, u32[]{:S(2)}) copy-start(f32[2,2,256,256]{3,2,1,0:T(8,128)S(1)} %collective-permute-done.2.recv_ref) | copy-start | bytes 3145732
  55.4 17.2 %collective-permute-start.4 = (f32[2,2,256,256]{3,2,1,0:T(8,128)}, f32[2,2,256,256]{3,2,1,0:T(8,128)S(1)}, u32[]{:S(2)}, u32[]{:S(2)}) collective-permute-start(f32[2,2,256,256]{3,2,1,0:T(8,128)} %get-tuple-element.12), channel_id=1, source_target_pairs={{0,1},{1,2},{2,3},{3,4},{4,5},{5,6},{6,7},{7,8},{8,9},{9,10},{10,1... | collective-permute-start | bytes 3145736 | tf_op jit(solution)/shard_map/ppermute | solution.py:19
  58.3 14.3 %copy-start = (f32[2,2,256,256]{3,2,1,0:T(8,128)}, f32[2,2,256,256]{3,2,1,0:T(8,128)S(1)}, u32[]{:S(2)}) copy-start(f32[2,2,256,256]{3,2,1,0:T(8,128)S(1)} %collective-permute-done.3.refs_2_) | copy-start | bytes 3145732
  72.6 1.0 %copy-start.1 = (f32[2,2,256,256]{3,2,1,0:T(8,128)}, f32[2,2,256,256]{3,2,1,0:T(8,128)S(1)}, u32[]{:S(2)}) copy-start(f32[2,2,256,256]{3,2,1,0:T(8,128)S(1)} %collective-permute-done.4.refs_3_) | copy-start | bytes 3145732

commit v2 on v0

v2 whole, which is shorter than its diff:
```python
import functools
import math

import jax
import jax.numpy as jnp
import numpy as np
from jax import lax
from jax.experimental import pallas as pl
from jax.experimental.pallas import tpu as pltpu
from jax.sharding import PartitionSpec as P

SPREAD_PHASE = 40.0
LANES = 128


def permute_along(block, axis, distance):
    devices = range(lax.axis_size(axis))
    route = [(i - distance, i) for i in devices if i - distance in devices]
    return lax.ppermute(block, axis, route)


def matrix_tables(width):
    counter = np.arange(width)
    angles = (counter[:, None] * counter[None, :] % width) * (2.0 * math.pi / width)
    wave = np.exp(-1j * angles) / math.sqrt(width)
    folded = ((counter + width // 2) % width - width // 2) / width
    phases = np.exp(-1j * SPREAD_PHASE * folded**2)
    spread = (np.conj(wave) * phases[None, :]) @ wave
    spread = (spread + spread.T) / 2
    stacked = np.stack([np.block([[t.real, t.imag], [-t.imag, t.real]]) for t in (spread, wave)])
    high = stacked.astype(jnp.bfloat16)
    low = (stacked - high.astype(np.float64)).astype(jnp.bfloat16)
    return jnp.asarray(high), jnp.asarray(low)


def split(value):
    high = value.astype(jnp.bfloat16)
    return high, (value - high.astype(jnp.float32)).astype(jnp.bfloat16)


VMEM = pl.BlockSpec(memory_space=pltpu.VMEM)
PARAMS = pltpu.CompilerParams(vmem_limit_bytes=24 * 2**20)


def on_chip(array):
    return pltpu.with_memory_space_constraint(array, pltpu.VMEM)


SMEM = pl.BlockSpec(memory_space=pltpu.SMEM)


def column_block(offset, window, length):
    block = jnp.minimum(offset // LANES, (length - window) // LANES - 1)
    return block, offset - block * LANES


def columns_at(tile_ref, s, c, rows, offset, window):
    block, shift = column_block(offset, window, tile_ref.shape[-1])
    lane = lax.broadcasted_iota(jnp.int32, (rows.size, LANES), 1)
    turned = []
    for j in range(window // LANES + 1):
        start = pl.multiple_of((block + j) * LANES, LANES)
        turned.append(pltpu.roll(tile_ref[s, c, rows, pl.ds(start, LANES)], LANES - shift, 1))
    return [jnp.where(lane < LANES - shift, turned[j], turned[j + 1]) for j in range(window // LANES)]


def subtract_at(tile_ref, s, c, rows, offset, piece):
    window = piece.shape[1]
    block, shift = column_block(offset, window, tile_ref.shape[-1])
    lane = lax.broadcasted_iota(jnp.int32, (rows.size, LANES), 1)
    parts = window // LANES
    turned = [pltpu.roll(piece[:, j * LANES : (j + 1) * LANES], shift, 1) for j in range(parts)]
    for j in range(parts + 1):
        start = pl.multiple_of((block + j) * LANES, LANES)
        above = turned[j - 1] if j > 0 else jnp.zeros_like(turned[0])
        here = turned[j] if j < parts else jnp.zeros_like(turned[0])
        columns = pl.ds(start, LANES)
        tile_ref[s, c, rows, columns] = tile_ref[s, c, rows, columns] - jnp.where(lane < shift, above, here)


def planes(ref):
    return [(s, c) for s in range(ref.shape[0]) for c in range(ref.shape[1])]


def pack_kernel(position, offsets, tile_ref, out_ref):
    _, _, tile, window = out_ref.shape
    for s, c in planes(out_ref):
        parts = columns_at(tile_ref, s, c, pl.ds(0, tile), offsets[position], window)
        for j, part in enumerate(parts):
            out_ref[s, c, :, j * LANES : (j + 1) * LANES] = part


def pack_windows(objects, offsets, position, window):
    shape = objects.shape[:3] + (window,)
    return pl.pallas_call(
        functools.partial(pack_kernel, position),
        in_specs=[SMEM, VMEM],
        out_specs=VMEM,
        out_shape=pltpu.VMEM(shape, jnp.float32),
        compiler_params=PARAMS,
        cost_estimate=pl.CostEstimate(flops=10**6, bytes_accessed=2**21, transcendentals=0),
        name="pack",
    )(offsets, objects)


def cmul(ar, ai, br, bi):
    return ar * br - ai * bi, ar * bi + ai * br


def cmul_conj(ar, ai, br, bi):
    return ar * br + ai * bi, ar * bi - ai * br


def window_kernel(position, x_offsets, y_offsets, modes, tile_ref, recv_ref, probe_ref, measured_ref,
                  high_ref, low_ref, state_ref, total_ref, ret_ref,
                  extended, win, left_high, left_low, right_high, right_low, entry, field):
    slices, parts, tile, window = recv_ref.shape
    x_offset, y_offset, mode = x_offsets[position], y_offsets[position], modes[position]
    offset = lax.rem(x_offset, 8)
    base = pl.multiple_of(x_offset - offset, 8)
    padded = window + 8

    for s, c in planes(recv_ref):
        for j, part in enumerate(columns_at(tile_ref, s, c, pl.ds(0, tile), y_offset, window)):
            extended[0:tile, j * LANES : (j + 1) * LANES] = part
        extended[tile : 2 * tile] = recv_ref[s, c]
        loaded = extended[pl.ds(base, padded), :]
        win[s, c] = pltpu.roll(loaded, padded - offset, 0)[:window]

    product = functools.partial(jnp.dot, preferred_element_type=jnp.float32)

    def transform(real, imag, table):
        left_high[:, 0:window], left_low[:, 0:window] = split(real)
        left_high[:, window:], left_low[:, window:] = split(imag)
        last = (product(left_high[...], high_ref[table]) + product(left_high[...], low_ref[table])
                + product(left_low[...], high_ref[table]))
        high, low = split(last[:, 0:window])
        right_high[0:window, 0:window] = high
        right_low[0:window, 0:window] = low
        right_high[window:, window:] = high
        right_low[window:, window:] = low
        high, low = split(last[:, window:])
        right_high[0:window, window:] = high
        right_low[0:window, window:] = low
        right_high[window:, 0:window] = -high
        right_low[window:, 0:window] = -low
        high, low = high_ref[table, 0:window], low_ref[table, 0:window]
        first = (product(high, right_high[...]) + product(high, right_low[...])
                 + product(low, right_high[...]))
        return first[:, 0:window], first[:, window:]

    def transform_conj(real, imag, table):
        real, imag = transform(real, -imag, table)
        return real, -imag

    def store_piece(s, piece):
        for c in range(parts):
            value = jnp.concatenate([piece[c], jnp.zeros((8, window), jnp.float32)], axis=0)
            extended[...] = jnp.zeros_like(extended)
            extended[pl.ds(base, padded), :] = pltpu.roll(value, offset, 0)
            ret_ref[s, c] = extended[tile : 2 * tile]
            subtract_at(total_ref, s, c, pl.ds(0, tile), y_offset, extended[0:tile])

    entry[0], entry[1] = transform(*cmul(probe_ref[mode, 0], probe_ref[mode, 1], win[0, 0], win[0, 1]), 0)
    fr, fi = transform(*cmul(entry[0], entry[1], win[1, 0], win[1, 1]), 1)
    residual = fr * fr + fi * fi - measured_ref[position]
    field[0], field[1] = transform_conj(residual * fr, residual * fi, 1)
    if position == 0:
        total_ref[...] = state_ref[...]
    store_piece(1, cmul_conj(entry[0], entry[1], field[0], field[1]))
    field[0], field[1] = transform_conj(*cmul_conj(win[1, 0], win[1, 1], field[0], field[1]), 0)
    store_piece(0, cmul_conj(probe_ref[mode, 0], probe_ref[mode, 1], field[0], field[1]))


def window_gradient(objects, total, received, probes, measured, tables, offsets, position):
    window = measured.shape[-1]
    parts = objects.shape[1]
    return pl.pallas_call(
        functools.partial(window_kernel, position),
        in_specs=[SMEM] * 3 + [VMEM] * 7,
        out_specs=[VMEM, VMEM],
        scratch_shapes=[
            pltpu.VMEM((objects.shape[2] + window + 8, window), jnp.float32),
            pltpu.VMEM(received.shape, jnp.float32),
            *[pltpu.VMEM((window, 2 * window), jnp.bfloat16)] * 2,
            *[pltpu.VMEM((2 * window, 2 * window), jnp.bfloat16)] * 2,
            pltpu.VMEM((parts, window, window), jnp.float32),
            pltpu.VMEM((parts, window, window), jnp.float32),
        ],
        out_shape=[pltpu.VMEM(objects.shape, jnp.float32), pltpu.VMEM(received.shape, jnp.float32)],
        compiler_params=PARAMS,
        input_output_aliases={9: 0} if position else {},
        cost_estimate=pl.CostEstimate(flops=6 * 10**9, bytes_accessed=6 * 2**20, transcendentals=0),
        name="window_gradient",
    )(*offsets, objects, received, probes, measured, *tables, total)


def subtract_kernel(position, offsets, piece_ref, state_ref, out_ref):
    del state_ref
    for s, c in planes(piece_ref):
        subtract_at(out_ref, s, c, pl.ds(0, piece_ref.shape[2]), offsets[position], piece_ref[s, c])


def subtract_window(total, piece, offsets, position):
    return pl.pallas_call(
        functools.partial(subtract_kernel, position),
        in_specs=[SMEM, VMEM, VMEM],
        out_specs=VMEM,
        out_shape=pltpu.VMEM(total.shape, jnp.float32),
        compiler_params=PARAMS,
        input_output_aliases={2: 0},
        cost_estimate=pl.CostEstimate(flops=10**6, bytes_accessed=2**21, transcendentals=0),
        name="subtract",
    )(offsets, piece, total)


def on_device(objects, probes, x_offsets, y_offsets, modes, measured):
    amount, window = measured.shape[0], measured.shape[-1]
    tables = [on_chip(t) for t in matrix_tables(window)]
    objects, probes, measured = on_chip(objects), on_chip(probes), on_chip(measured)
    left_offsets = permute_along(y_offsets, "lat", 1)
    received = [
        on_chip(permute_along(pack_windows(objects, left_offsets, p, window), "lat", -1))
        for p in range(amount)
    ]
    total, returned = objects, []
    for p in range(amount):
        total, piece = window_gradient(
            objects, total, received[p], probes, measured, tables, (x_offsets, y_offsets, modes), p)
        returned.append(on_chip(permute_along(piece, "lat", 1)))
    for p in range(amount):
        total = subtract_window(total, returned[p], left_offsets, p)
    return total


def solution(mesh):
    in_specs = (
        P(None, None, ("groups", "lat"), None),
        P("groups", None, None, None),
        P(("groups", "lat")),
        P(("groups", "lat")),
        P(("groups", "lat")),
        P(("groups", "lat"), None, None),
    )
    out_specs = P(None, None, ("groups", "lat"), None)
    return jax.shard_map(
        on_device, mesh=mesh, in_specs=in_specs, out_specs=out_specs, check_vma=False
    )
```

time: 272 us -> 62.7 us (0.23); the launches traced: 267 us -> 61.7 us
  matrix products: 90.6 us -> 0 us
  waiting for transfers between devices: 86.3 us -> 28.3 us
  local copies, waits for them, and re-layouts: 50.1 us -> 4.24 us
  other arithmetic: 25.8 us -> 0 us
  Pallas kernels: 0 us -> 16.8 us
  loops' own time: 7.97 us -> 0 us
  starting transfers between devices: 5.95 us -> 12.2 us
    dot_general x48 -> x0, matrix products: 90.6 us -> none  [the longest x6 11.6 us: fourier_pair(): jnp.einsum('pjk,kl->pjl', real_part, signed, precision=highest)]
    ppermute x2 -> x5, waiting for transfers between devices: 86.3 us -> 28.3 us  [permute_along(): return lax.ppermute(block, axis, route)]
    dynamic_update_slice x2 -> x0, local copies, waits for them, and re-layouts: 24 us -> none  [add_window(): return lax.dynamic_update_slice(buffer, current + pieces[i], corner)]
    pallas_call x0 -> x6, Pallas kernels: none -> 16.8 us  [the longest x2 12.7 us: window_gradient(): pl.pallas_call(functools.partial(window_kernel, position), in_specs=[SMEM...]
    gather x10 -> x0, local copies, waits for them, and re-layouts: 9.92 us -> none
    concatenate x2 -> x0, other arithmetic: 8.42 us -> none  [the longest x1 8.35 us: on_device(): extended = jnp.concatenate([objects, neighbour], axis=2)]
    another operation x2 -> x0, loops' own time: 7.97 us -> none  [the longest x1 7.51 us: on_device(): buffer = lax.fori_loop(0, amount, add_window, jnp.zeros_like(extended))]
    sub x2 -> x0, other arithmetic: 7.4 us -> none  [the longest x1 5.73 us: on_device(): return objects - descent_rate * gradient]
  transfers between devices with their start and end apart: 2 -> 5, of which waited for: 2 -> 5; matrix products, arithmetic and copies ran while one was open for 3% -> 0% of each run, Pallas kernels for 0% -> 24%
where the time goes in v2:
time: 62.7 us; the launch traced here: 61.7 us
  waiting for transfers between devices  28.3 us (45%)
  Pallas kernels  16.8 us (27%)
  starting transfers between devices  12.2 us (19%)
  local copies, waits for them, and re-layouts  4.24 us (7%)
    ppermute x5, waiting for transfers between devices, permute_along(): return lax.ppermute(block, axis, route)  28.3 us
    pallas_call x2, Pallas kernels, window_gradient(): pl.pallas_call(functools.partial(window_kernel, position), in_specs=[SMEM...  12.7 us
    ppermute x5, starting transfers between devices, permute_along(): return lax.ppermute(block, axis, route)  12.2 us
    unnamed x19, local copies, waits for them, and re-layouts  4.24 us
    pallas_call x2, Pallas kernels, subtract_window(): pl.pallas_call(functools.partial(subtract_kernel, position), in_specs=[SM...  2.05 us
    pallas_call x2, Pallas kernels, pack_windows(): pl.pallas_call(functools.partial(pack_kernel, position), in_specs=[SMEM,...  2.04 us
  transfers between devices with their start and end apart: 5, of which 5 were waited for; matrix products, arithmetic and copies ran while one was open for 0% of the time, Pallas kernels for 24%

profile of v2, /device:TPU:16, one launch (start us, length us, event | category | flops | bytes accessed | tf_op | source)
XLA Modules:
  0.0 61.7 jit_solution(11966638032617892996)
XLA Ops:
  0.0 1.9 %collective-permute-start = (s32[2]{0:T(128)}, s32[2]{0:T(128)S(1)}, u32[]{:S(2)}, u32[]{:S(2)}) collective-permute-start(s32[2]{0:T(128)} %y_offsets.3), channel_id=1, source_target_pairs={{0,1},{1,2},{2,3},{3,4},{4,5},{5,6},{6,7},{7,8},{8,9},{9,10},{10,1... | collective-permute-start | bytes 32 | tf_op jit(solution)/shard_map/ppermute | solution.py:19
  1.9 4.0 %collective-permute-done.offsets = s32[2]{0:T(128)S(1)} collective-permute-done((s32[2]{0:T(128)}, s32[2]{0:T(128)S(1)}, u32[]{:S(2)}, u32[]{:S(2)}) %collective-permute-start) | collective-permute-done | bytes 40 | tf_op jit(solution)/shard_map/ppermute | solution.py:19
  5.9 2.2 %copy-done = f32[2,2,256,1024]{3,2,1,0:T(8,128)S(1)} copy-done((f32[2,2,256,1024]{3,2,1,0:T(8,128)S(1)}, f32[2,2,256,1024]{3,2,1,0:T(8,128)}, u32[]{:S(2)}) %copy-start) | copy-done | bytes 4194328
  8.1 0.0 copy-start.5
  8.1 0.0 copy-start.6
  8.1 0.0 copy-start.7
  8.1 0.0 copy-start.8
  8.2 1.0 %pack.3 = f32[2,2,256,256]{3,2,1,0:T(8,128)S(1)} custom-call(s32[2]{0:T(128)S(1)} %collective-permute-done.offsets, f32[2,2,256,1024]{3,2,1,0:T(8,128)S(1)} %copy-done), custom_call_target="tpu_custom_call" | custom-call | flops 1000000 | bytes 2097152 | tf_op jit(solution)/shard_map/pack/pallas_call | solution.py:95
  9.2 2.2 %collective-permute-start.2 = (f32[2,2,256,256]{3,2,1,0:T(8,128)S(1)}, f32[2,2,256,256]{3,2,1,0:T(8,128)S(1)}, u32[]{:S(2)}, u32[]{:S(2)}) collective-permute-start(f32[2,2,256,256]{3,2,1,0:T(8,128)S(1)} %pack.3), channel_id=1, source_target_pairs={{1,0},{2,1},{3,2},{4,3},{5,4},{6,5},{7,6},{8,7},{9,8},{10,9},{11,1... | collective-permute-start | bytes 3145736 | tf_op jit(solution)/shard_map/ppermute | solution.py:19
  11.4 1.0 %pack.2 = f32[2,2,256,256]{3,2,1,0:T(8,128)S(1)} custom-call(s32[2]{0:T(128)S(1)} %collective-permute-done.offsets, f32[2,2,256,1024]{3,2,1,0:T(8,128)S(1)} %copy-done), custom_call_target="tpu_custom_call" | custom-call | flops 1000000 | bytes 2097152 | tf_op jit(solution)/shard_map/pack/pallas_call | solution.py:95
  12.4 2.5 %collective-permute-start.1 = (f32[2,2,256,256]{3,2,1,0:T(8,128)S(1)}, f32[2,2,256,256]{3,2,1,0:T(8,128)S(1)}, u32[]{:S(2)}, u32[]{:S(2)}) collective-permute-start(f32[2,2,256,256]{3,2,1,0:T(8,128)S(1)} %pack.2), channel_id=1, source_target_pairs={{1,0},{2,1},{3,2},{4,3},{5,4},{6,5},{7,6},{8,7},{9,8},{10,9},{11,1... | collective-permute-start | bytes 3145736 | tf_op jit(solution)/shard_map/ppermute | solution.py:19
  14.9 8.7 %collective-permute-done.2.recv_ref = f32[2,2,256,256]{3,2,1,0:T(8,128)S(1)} collective-permute-done((f32[2,2,256,256]{3,2,1,0:T(8,128)S(1)}, f32[2,2,256,256]{3,2,1,0:T(8,128)S(1)}, u32[]{:S(2)}, u32[]{:S(2)}) %collective-permute-start.2) | collective-permute-done | bytes 1048608 | tf_op jit(solution)/shard_map/ppermute | solution.py:19
  23.7 0.0 copy-done.1
  23.7 0.0 copy-done.2
  23.7 6.5 %window_gradient.2 = (f32[2,2,256,1024]{3,2,1,0:T(8,128)S(1)}, f32[2,2,256,256]{3,2,1,0:T(8,128)S(1)}) custom-call(s32[2]{0:T(128)S(1)} %copy-done.5, s32[2]{0:T(128)S(1)} %copy-done.4, s32[2]{0:T(128)S(1)} %copy-done.6, f32[2,2,256,1024]{3,2,1,0:T(8,128)S(1)} %copy-done.1, f32[2,2,256,256]{3,2,1,0:T(8,128)S(1)} %collective-permute-done.2.recv_ref, ...), custom_call_target="tpu_custom_call" | custom-call | flops 6000000000 | bytes 6291456 | tf_op jit(solution)/shard_map/window_gradient/pallas_call | solution.py:178
  30.2 2.8 %collective-permute-start.4 = (f32[2,2,256,256]{3,2,1,0:T(8,128)S(1)}, f32[2,2,256,256]{3,2,1,0:T(8,128)S(1)}, u32[]{:S(2)}, u32[]{:S(2)}) collective-permute-start(f32[2,2,256,256]{3,2,1,0:T(8,128)S(1)} %get-tuple-element.11), channel_id=1, source_target_pairs={{0,1},{1,2},{2,3},{3,4},{4,5},{5,6},{6,7},{7,8},{8,9},{9,10},{10,1... | collective-permute-start | bytes 3145736 | tf_op jit(solution)/shard_map/ppermute | solution.py:19
  33.0 1.9 %collective-permute-done.1.recv_ref = f32[2,2,256,256]{3,2,1,0:T(8,128)S(1)} collective-permute-done((f32[2,2,256,256]{3,2,1,0:T(8,128)S(1)}, f32[2,2,256,256]{3,2,1,0:T(8,128)S(1)}, u32[]{:S(2)}, u32[]{:S(2)}) %collective-permute-start.1) | collective-permute-done | bytes 1048608 | tf_op jit(solution)/shard_map/ppermute | solution.py:19
  35.0 6.3 %window_gradient.3 = (f32[2,2,256,1024]{3,2,1,0:T(8,128)S(1)}, f32[2,2,256,256]{3,2,1,0:T(8,128)S(1)}) custom-call(s32[2]{0:T(128)S(1)} %copy-done.5, s32[2]{0:T(128)S(1)} %copy-done.4, s32[2]{0:T(128)S(1)} %copy-done.6, f32[2,2,256,1024]{3,2,1,0:T(8,128)S(1)} %copy-done.1, ...), custom_call_target="tpu_custom_call", output_to_operand_aliasing={{0}: (9, {})} | custom-call | flops 6000000000 | bytes 6291456 | tf_op jit(solution)/shard_map/window_gradient/pallas_call | solution.py:178
  41.2 2.8 %collective-permute-start.3 = (f32[2,2,256,256]{3,2,1,0:T(8,128)S(1)}, f32[2,2,256,256]{3,2,1,0:T(8,128)S(1)}, u32[]{:S(2)}, u32[]{:S(2)}) collective-permute-start(f32[2,2,256,256]{3,2,1,0:T(8,128)S(1)} %get-tuple-element.10), channel_id=1, source_target_pairs={{0,1},{1,2},{2,3},{3,4},{4,5},{5,6},{6,7},{7,8},{8,9},{9,10},{10,1... | collective-permute-start | bytes 3145736 | tf_op jit(solution)/shard_map/ppermute | solution.py:19
  44.0 3.4 %collective-permute-done.4.piece_ref = f32[2,2,256,256]{3,2,1,0:T(8,128)S(1)} collective-permute-done((f32[2,2,256,256]{3,2,1,0:T(8,128)S(1)}, f32[2,2,256,256]{3,2,1,0:T(8,128)S(1)}, u32[]{:S(2)}, u32[]{:S(2)}) %collective-permute-start.4) | collective-permute-done | bytes 1048608 | tf_op jit(solution)/shard_map/ppermute | solution.py:19
  47.4 1.0 %subtract.2.state_ref = f32[2,2,256,1024]{3,2,1,0:T(8,128)S(1)} custom-call(s32[2]{0:T(128)S(1)} %collective-permute-done.offsets, f32[2,2,256,256]{3,2,1,0:T(8,128)S(1)} %collective-permute-done.4.piece_ref, f32[2,2,256,1024]{3,2,1,0:T(8,128)S(1)} %get-tuple-element.12.state_ref), custom_call_target="tpu_custom_call", output_to_operand_aliasing={{}: (2, {})} | custom-call | flops 1000000 | bytes 2097152 | tf_op jit(solution)/shard_map/subtract/pallas_call | solution.py:205
  48.4 10.2 %collective-permute-done.3.piece_ref = f32[2,2,256,256]{3,2,1,0:T(8,128)S(1)} collective-permute-done((f32[2,2,256,256]{3,2,1,0:T(8,128)S(1)}, f32[2,2,256,256]{3,2,1,0:T(8,128)S(1)}, u32[]{:S(2)}, u32[]{:S(2)}) %collective-permute-start.3) | collective-permute-done | bytes 1048608 | tf_op jit(solution)/shard_map/ppermute | solution.py:19
  58.6 1.0 %subtract.3 = f32[2,2,256,1024]{3,2,1,0:T(8,128)S(1)} custom-call(s32[2]{0:T(128)S(1)} %collective-permute-done.offsets, f32[2,2,256,256]{3,2,1,0:T(8,128)S(1)} %collective-permute-done.3.piece_ref, f32[2,2,256,1024]{3,2,1,0:T(8,128)S(1)} %subtract.2.state_ref), custom_call_target="tpu_custom_call", output_to_operand_aliasing={{}: (2, {})} | custom-call | flops 1000000 | bytes 2097152 | tf_op jit(solution)/shard_map/subtract/pallas_call | solution.py:205
  59.7 2.0 %copy.15 = f32[2,2,256,1024]{3,2,1,0:T(8,128)} copy(f32[2,2,256,1024]{3,2,1,0:T(8,128)S(1)} %subtract.3) | data formatting | bytes 8388608
  (11 shorter events, 0.0 us)
Async XLA Ops:
  0.0 5.9 %collective-permute-start = (s32[2]{0:T(128)}, s32[2]{0:T(128)S(1)}, u32[]{:S(2)}, u32[]{:S(2)}) collective-permute-start(s32[2]{0:T(128)} %y_offsets.3), channel_id=1, source_target_pairs={{0,1},{1,2},{2,3},{3,4},{4,5},{5,6},{6,7},{7,8},{8,9},{9,10},{10,1... | collective-permute-start | bytes 32 | tf_op jit(solution)/shard_map/ppermute | solution.py:19
  5.9 2.2 %copy-start = (f32[2,2,256,1024]{3,2,1,0:T(8,128)S(1)}, f32[2,2,256,1024]{3,2,1,0:T(8,128)}, u32[]{:S(2)}) copy-start(f32[2,2,256,1024]{3,2,1,0:T(8,128)} %tile_ref.7) | copy-start | bytes 12582916
  8.1 15.6 %copy-start.1 = (f32[2,2,256,1024]{3,2,1,0:T(8,128)S(1)}, f32[2,2,256,1024]{3,2,1,0:T(8,128)}, u32[]{:S(2)}) copy-start(f32[2,2,256,1024]{3,2,1,0:T(8,128)} %tile_ref.7) | copy-start | bytes 12582916
  8.1 15.6 %copy-start.2 = (f32[2,2,256,256]{3,2,1,0:T(8,128)S(1)}, f32[2,2,256,256]{3,2,1,0:T(8,128)}, u32[]{:S(2)}) copy-start(f32[2,2,256,256]{3,2,1,0:T(8,128)} %probe_ref.3) | copy-start | bytes 3145732
  8.1 15.6 %copy-start.3 = (f32[2,256,256]{2,1,0:T(8,128)S(1)}, f32[2,256,256]{2,1,0:T(8,128)}, u32[]{:S(2)}) copy-start(f32[2,256,256]{2,1,0:T(8,128)} %measured_ref.3) | copy-start | bytes 1572868
  8.1 15.6 %copy-start.4 = (s32[2]{0:T(128)S(1)}, s32[2]{0:T(128)}, u32[]{:S(2)}) copy-start(s32[2]{0:T(128)} %y_offsets.3) | copy-start | bytes 28
  8.1 15.6 %copy-start.5 = (s32[2]{0:T(128)S(1)}, s32[2]{0:T(128)}, u32[]{:S(2)}) copy-start(s32[2]{0:T(128)} %x_offsets.3) | copy-start | bytes 28
  8.1 15.6 %copy-start.6 = (s32[2]{0:T(128)S(1)}, s32[2]{0:T(128)}, u32[]{:S(2)}) copy-start(s32[2]{0:T(128)} %modes.3) | copy-start | bytes 28
  8.1 15.6 %copy-start.7 = (bf16[2,512,512]{2,1,0:T(8,128)(2,1)S(1)}, bf16[2,512,512]{2,1,0:T(8,128)(2,1)}, u32[]{:S(2)}) copy-start(bf16[2,512,512]{2,1,0:T(8,128)(2,1)} %constant.5.clone.low_ref) | copy-start | bytes 3145732
  8.1 15.6 %copy-start.8 = (bf16[2,512,512]{2,1,0:T(8,128)(2,1)S(1)}, bf16[2,512,512]{2,1,0:T(8,128)(2,1)}, u32[]{:S(2)}) copy-start(bf16[2,512,512]{2,1,0:T(8,128)(2,1)} %constant.4.clone.high_ref) | copy-start | bytes 3145732
  9.2 14.5 %collective-permute-start.2 = (f32[2,2,256,256]{3,2,1,0:T(8,128)S(1)}, f32[2,2,256,256]{3,2,1,0:T(8,128)S(1)}, u32[]{:S(2)}, u32[]{:S(2)}) collective-permute-start(f32[2,2,256,256]{3,2,1,0:T(8,128)S(1)} %pack.3), channel_id=1, source_target_pairs={{1,0},{2,1},{3,2},{4,3},{5,4},{6,5},{7,6},{8,7},{9,8},{10,9},{11,1... | collective-permute-start | bytes 3145736 | tf_op jit(solution)/shard_map/ppermute | solution.py:19
  12.4 22.5 %collective-permute-start.1 = (f32[2,2,256,256]{3,2,1,0:T(8,128)S(1)}, f32[2,2,256,256]{3,2,1,0:T(8,128)S(1)}, u32[]{:S(2)}, u32[]{:S(2)}) collective-permute-start(f32[2,2,256,256]{3,2,1,0:T(8,128)S(1)} %pack.2), channel_id=1, source_target_pairs={{1,0},{2,1},{3,2},{4,3},{5,4},{6,5},{7,6},{8,7},{9,8},{10,9},{11,1... | collective-permute-start | bytes 3145736 | tf_op jit(solution)/shard_map/ppermute | solution.py:19
  30.2 17.2 %collective-permute-start.4 = (f32[2,2,256,256]{3,2,1,0:T(8,128)S(1)}, f32[2,2,256,256]{3,2,1,0:T(8,128)S(1)}, u32[]{:S(2)}, u32[]{:S(2)}) collective-permute-start(f32[2,2,256,256]{3,2,1,0:T(8,128)S(1)} %get-tuple-element.11), channel_id=1, source_target_pairs={{0,1},{1,2},{2,3},{3,4},{4,5},{5,6},{6,7},{7,8},{8,9},{9,10},{10,1... | collective-permute-start | bytes 3145736 | tf_op jit(solution)/shard_map/ppermute | solution.py:19
  41.2 17.4 %collective-permute-start.3 = (f32[2,2,256,256]{3,2,1,0:T(8,128)S(1)}, f32[2,2,256,256]{3,2,1,0:T(8,128)S(1)}, u32[]{:S(2)}, u32[]{:S(2)}) collective-permute-start(f32[2,2,256,256]{3,2,1,0:T(8,128)S(1)} %get-tuple-element.10), channel_id=1, source_target_pairs={{0,1},{1,2},{2,3},{3,4},{4,5},{5,6},{6,7},{7,8},{8,9},{9,10},{10,1... | collective-permute-start | bytes 3145736 | tf_op jit(solution)/shard_map/ppermute | solution.py:19
